TPU v7x, 256 devices: a whole 4x4x8 slice. The times are simulated.
256 devices in a mesh: wide: 16 (over y, x), narrow: 16 (over z, core).
Axes of the slice: x: 4, y: 4, z: 8, core: 2. Of those that a mesh axis runs over, the one named last changes fastest.
Arguments:
- charges: bfloat16 [4096, 256, 128], P(('wide', 'narrow')), may hold values from -6 to 6
- pairs_first: int32 [16384, 4], P(('wide', 'narrow')), may hold values from 0 to 15, as said below
- pairs_second: int32 [16384, 4], P(('wide', 'narrow')), may hold values from 0 to 15, as said below
- pairs_third: int32 [16384, 4], P(('wide', 'narrow')), may hold values from 0 to 15, as said below
- matrices_first: bfloat16 [2048, 256, 256], P(('wide', 'narrow')), may hold values from -0.21875 to 0.21875
- matrices_second: bfloat16 [2048, 256, 256], P(('wide', 'narrow')), may hold values from -0.21875 to 0.21875
- matrices_third: bfloat16 [2048, 256, 256], P(('wide', 'narrow')), may hold values from -0.21875 to 0.21875
- box_owner: int32 [16, 16, 16], P('wide', 'narrow'), may hold values from 0 to 15, as said below
Outputs:
- potentials: bfloat16 [4096, 256, 128], P(('wide', 'narrow'))
Inputs may be any that keep to these rules, and one draw needn't show every extreme that they name: `pairs_first`: each device's 64 rows hold a source box and a target box below 16, a matrix below 8 and a live flag 0 or 1; live rows come before the others; in every list some device has all rows live. `pairs_second`: same form as pairs_first. `pairs_third`: same form as pairs_first. `box_owner`: for each narrow index, every wide index hands 0 or 2 of its boxes to each owner, and each owner receives exactly 16 boxes.
All inputs are finite; a program needn't handle non-finite values.
Results may differ from a plain program's by a relative error of at most 0.0057.
Values may be sent and summed in bfloat16 or wider, within the bound.
A program may use at most 64 MiB of HBM per device.

v0:
```python
import functools

import jax
import jax.numpy as jnp
from jax import lax
from jax.experimental import pallas as pl
from jax.experimental.pallas import tpu as pltpu
from jax.sharding import PartitionSpec as P

MESH = pl.DeviceIdType.MESH
R = 256
RHS = 128
BOX = 16
PAIRS = 64
TRANS = 8
GROUP = 16
PIECE = R // GROUP
CHUNKS = 2
HALF = RHS // 2
TILES = BOX // 2
UNROLL = 8
BF = jnp.bfloat16
F32 = jnp.float32


def far_first(e):
    return 8 + jnp.where(lax.rem(e, 2) == 1, -((e + 1) // 2), e // 2)


def torus_first(w, e):
    return lax.rem(w + far_first(e), GROUP)


def column_of(row, eye):
    return jnp.sum(jnp.where(eye, row, 0), axis=1, keepdims=True)


def list_table(rows):
    line = lax.broadcasted_iota(jnp.int32, (PAIRS, PAIRS), 0)
    lane = lax.broadcasted_iota(jnp.int32, (PAIRS, PAIRS), 1)
    eye = line == lane
    source, target, matrix, live = (rows[i : i + 1, :] for i in range(4))
    place = lax.broadcasted_iota(jnp.int32, (1, PAIRS), 1)
    group = jnp.where(live > 0, target, BOX)
    key = group * PAIRS + place
    swap = (source ^ target) & 1
    word = (source // 2 + TILES * swap) | (matrix << 4)
    key_col = column_of(key, eye)
    word_col = column_of(word, eye)
    group_col = key_col // PAIRS
    before = key < key_col
    rank_col = jnp.sum(jnp.where(before, 1, 0), axis=1, keepdims=True)
    follows = jnp.sum(jnp.where(before & (group == group_col), 1, 0), axis=1, keepdims=True)
    word_col = word_col | jnp.where((follows > 0) & (group_col < BOX), 1 << 7, 0)
    ordered = jnp.sum(jnp.where(rank_col == lane, word_col, 0), axis=0, keepdims=True)
    upto = jnp.sum(jnp.where(group_col <= lane, 1, 0), axis=0, keepdims=True)
    count = jnp.sum(jnp.where(group_col == lane, 1, 0), axis=0, keepdims=True)
    last = jnp.where(count > 0, upto - 1, PAIRS)
    return ordered, last


def send_table(row):
    line = lax.broadcasted_iota(jnp.int32, (BOX, BOX), 0)
    lane = lax.broadcasted_iota(jnp.int32, (BOX, BOX), 1)
    eye = line == lane
    col = column_of(row, eye)
    earlier = jnp.sum(jnp.where((row == col) & (lane < line), 1, 0), axis=1, keepdims=True)
    slot = 2 * col + earlier
    wide = lax.broadcasted_iota(jnp.int32, (BOX, PAIRS), 1)
    box = lax.broadcasted_iota(jnp.int32, (BOX, PAIRS), 0)
    return jnp.sum(jnp.where(slot == wide, box, 0), axis=0, keepdims=True)


def arrival_table(owners, me):
    hands = jnp.sum(jnp.where(owners == me, 1, 0), axis=1, keepdims=True)
    line = lax.broadcasted_iota(jnp.int32, (GROUP, GROUP), 0)
    lane = lax.broadcasted_iota(jnp.int32, (GROUP, GROUP), 1)
    filled = jnp.where(hands > 0, 1, 0)
    filled_row = jnp.sum(jnp.where(line == lane, filled, 0), axis=0, keepdims=True)
    rank = jnp.sum(jnp.where(lane < line, filled_row, 0), axis=1, keepdims=True)
    wide = lax.broadcasted_iota(jnp.int32, (GROUP, PAIRS), 1)
    index = lax.broadcasted_iota(jnp.int32, (GROUP, PAIRS), 0)
    return jnp.sum(jnp.where((filled > 0) & (rank == wide), index, 0), axis=0, keepdims=True)


def swap_halves(x):
    return pltpu.roll(x, HALF, 1)


def body(
    charges, pairs_a, pairs_b, pairs_c, mats_a, mats_b, mats_c, owner, out,
    c_v, m_a, m_b, m_c, lists, own_in, own_all, tables, table_s,
    x_v, p_v, stage_a, recv_a, stage_b, recv_b, stage_c, recv_c, out_v,
    in_sem, small_sem, table_sem, out_sem, own_send, own_recv, send_sem, recv_sem,
):
    w = lax.axis_index("wide")
    n = lax.axis_index("narrow")
    barrier = pltpu.get_barrier_semaphore()

    def greet(d, carry):
        pl.semaphore_signal(
            barrier, inc=1, device_id=(w, lax.rem(n + d, GROUP)), device_id_type=MESH
        )
        pl.semaphore_signal(
            barrier, inc=1, device_id=(lax.rem(w + d, GROUP), n), device_id_type=MESH
        )
        return carry

    small = [
        pltpu.make_async_copy(src, lists.at[i], small_sem.at[i])
        for i, src in enumerate((pairs_a, pairs_b, pairs_c))
    ]
    small.append(pltpu.make_async_copy(owner, own_in, small_sem.at[3]))
    large = [
        pltpu.make_async_copy(src, dst, in_sem.at[i])
        for i, (src, dst) in enumerate(
            ((charges, c_v), (mats_a, m_a), (mats_b, m_b), (mats_c, m_c))
        )
    ]
    for copy in small:
        copy.start()
    for copy in large:
        copy.start()
    lax.fori_loop(1, GROUP, greet, 0)

    for copy in small:
        copy.wait()
    table_copies = [
        pltpu.make_async_copy(tables.at[i], table_s.at[i], table_sem.at[i]) for i in range(5)
    ]
    for level in range(3):
        ordered, last = list_table(lists[level])
        tables[level, 0:1, 0:PAIRS] = ordered
        tables[level, 1:2, 0:PAIRS] = last
        table_copies[level].start()
    tables[3, 0:1, 0:PAIRS] = send_table(own_in[...])
    table_copies[3].start()
    own_all[w] = jnp.full((8, 128), -1, jnp.int32)
    own_all[w, 0:1, 0:BOX] = own_in[...]
    p_v[PAIRS] = jnp.zeros((R, RHS), BF)
    low = lax.broadcasted_iota(jnp.int32, (R, RHS), 1) < HALF

    def narrow_copy(stage, recv, phase, chunk, d):
        to = lax.rem(n + d, GROUP)
        return pltpu.make_async_remote_copy(
            src_ref=stage.at[chunk, to],
            dst_ref=recv.at[chunk, n],
            send_sem=send_sem.at[phase, chunk, d],
            recv_sem=recv_sem.at[phase, chunk, d],
            device_id=(w, to),
            device_id_type=MESH,
        )

    def wide_copy(stage, recv, phase, chunk, d):
        to = lax.rem(w + d, GROUP)
        return pltpu.make_async_remote_copy(
            src_ref=stage.at[chunk, to],
            dst_ref=recv.at[chunk, w],
            send_sem=send_sem.at[phase, chunk, d],
            recv_sem=recv_sem.at[phase, chunk, d],
            device_id=(to, n),
            device_id_type=MESH,
        )

    copies = {
        0: functools.partial(narrow_copy, stage_a, recv_a, 0),
        1: functools.partial(wide_copy, stage_b, recv_b, 1),
        2: functools.partial(wide_copy, stage_c, recv_c, 2),
    }
    stages = {0: stage_a, 1: stage_b}
    received = {0: recv_a, 1: recv_b, 2: recv_c}

    def owner_copy(d):
        to = lax.rem(w + d, GROUP)
        return pltpu.make_async_remote_copy(
            src_ref=own_all.at[w],
            dst_ref=own_all.at[w],
            send_sem=own_send.at[d],
            recv_sem=own_recv.at[d],
            device_id=(to, n),
            device_id_type=MESH,
        )

    def load_charges(chunk):
        def one(i, carry):
            first = c_v[2 * i].astype(F32)
            second = c_v[2 * i + 1].astype(F32)
            if chunk == 0:
                here = jnp.where(low, first, swap_halves(second))
                there = jnp.where(low, second, swap_halves(first))
            else:
                here = jnp.where(low, swap_halves(first), second)
                there = jnp.where(low, swap_halves(second), first)
            x_v[i] = here.astype(BF)
            x_v[TILES + i] = there.astype(BF)
            return carry

        lax.fori_loop(0, TILES, one, 0)

    def load_received(recv, chunk):
        def one(i, carry):
            tile = recv[chunk, :, i].reshape(R, RHS)
            x_v[i] = tile
            x_v[TILES + i] = swap_halves(tile.astype(F32)).astype(BF)
            return carry

        lax.fori_loop(0, TILES, one, 0)

    def translate(level):
        matrices = (m_a, m_b, m_c)[level]

        def one(r, acc):
            word = table_s[level, 0, r]
            product = jnp.dot(
                matrices[(word >> 4) & 7], x_v[word & 15], preferred_element_type=F32
            )
            acc = jnp.where((word >> 7) & 1 == 1, acc, 0.0) + product
            p_v[r] = acc.astype(BF)
            return acc

        lax.fori_loop(0, PAIRS, one, jnp.zeros((R, RHS), F32), unroll=UNROLL)

    def assemble(level, chunk):
        stage = stages[level]

        def one(i, carry):
            first = p_v[table_s[level, 1, 2 * i]]
            second = p_v[table_s[level, 1, 2 * i + 1]]
            tile = jnp.where(low, first.astype(F32), second.astype(F32)).astype(BF)
            stage[chunk, :, i] = tile.reshape(GROUP, PIECE, RHS)
            return carry

        lax.fori_loop(0, TILES, one, 0)

    def send(level, chunk):
        def one(e, carry):
            copies[level](chunk, far_first(e)).start()
            return carry

        lax.fori_loop(0, GROUP - 1, one, 0)
        me = n if level == 0 else w
        received[level][chunk, me] = stages[level][chunk, me]

    def arrive(level, chunk):
        def one(d, carry):
            copies[level](chunk, d).wait_recv()
            return carry

        lax.fori_loop(1, GROUP, one, 0)

    def sent(level, chunk):
        def one(d, carry):
            copies[level](chunk, d).wait_send()
            return carry

        lax.fori_loop(1, GROUP, one, 0)

    def packet(chunk, to):
        halves = []
        for c in range(2):
            box = table_s[3, 0, 2 * to + c]
            rows = p_v[table_s[2, 1, box]].astype(F32)
            halves.append(jnp.where(box & 1 == c, rows, swap_halves(rows)))
        stage_c[chunk, to] = jnp.where(low, halves[0], halves[1]).astype(BF)

    def hand_over(chunk):
        def one(e, carry):
            d = far_first(e)
            packet(chunk, lax.rem(w + d, GROUP))
            copies[2](chunk, d).start()
            return carry

        lax.fori_loop(0, GROUP - 1, one, 0)
        packet(chunk, w)
        recv_c[chunk, w] = stage_c[chunk, w]

    large[0].wait()
    load_charges(0)
    table_copies[0].wait()
    large[1].wait()
    translate(0)
    assemble(0, 0)
    pl.semaphore_wait(barrier, 2 * (GROUP - 1))
    send(0, 0)

    def give(d, carry):
        owner_copy(d).start()
        return carry

    lax.fori_loop(1, GROUP, give, 0)
    load_charges(1)
    translate(0)
    assemble(0, 1)
    send(0, 1)
    for copy in table_copies[1:4]:
        copy.wait()
    large[2].wait()
    large[3].wait()

    def taken(d, carry):
        owner_copy(d).wait()
        return carry

    lax.fori_loop(1, GROUP, taken, 0)
    tables[4, 0:1, 0:PAIRS] = arrival_table(own_all[:, 0, 0:BOX], w)
    table_copies[4].start()
    table_copies[4].wait()

    arrive(0, 0)
    load_received(recv_a, 0)
    translate(1)
    assemble(1, 0)
    send(1, 0)

    arrive(1, 0)
    load_received(recv_b, 0)
    translate(2)
    hand_over(0)

    arrive(0, 1)
    load_received(recv_a, 1)
    translate(1)
    assemble(1, 1)
    send(1, 1)

    arrive(1, 1)
    load_received(recv_b, 1)
    translate(2)
    hand_over(1)

    for level in range(2):
        for chunk in range(CHUNKS):
            sent(level, chunk)
    arrive(2, 0)
    arrive(2, 1)

    def place(j):
        return pltpu.make_async_copy(
            out_v.at[pl.ds(2 * j, 2)], out.at[pl.ds(2 * j, 2)], out_sem.at[j]
        )

    def finish(j, carry):
        origin = table_s[4, 0, j]
        left = recv_c[0, origin].astype(F32)
        right = recv_c[1, origin].astype(F32)
        out_v[2 * j] = jnp.where(low, left, swap_halves(right)).astype(BF)
        out_v[2 * j + 1] = jnp.where(low, swap_halves(left), right).astype(BF)
        place(j).start()
        return carry

    lax.fori_loop(0, TILES, finish, 0)

    def placed(j, carry):
        place(j).wait()
        return carry

    lax.fori_loop(0, TILES, placed, 0)
    for chunk in range(CHUNKS):
        sent(2, chunk)


def per_device(charges, pairs_a, pairs_b, pairs_c, mats_a, mats_b, mats_c, box_owner):
    any_space = pl.BlockSpec(memory_space=pl.ANY)
    flops = 2 * 3 * PAIRS * R * R * RHS
    return pl.pallas_call(
        body,
        out_shape=jax.ShapeDtypeStruct(charges.shape, charges.dtype),
        in_specs=[any_space] * 8,
        out_specs=any_space,
        scratch_shapes=[
            pltpu.VMEM((BOX, R, RHS), BF),
            *[pltpu.VMEM((TRANS, R, R), BF)] * 3,
            pltpu.VMEM((3, 4, PAIRS), jnp.int32),
            pltpu.VMEM((1, BOX), jnp.int32),
            pltpu.VMEM((GROUP, 8, 128), jnp.int32),
            pltpu.VMEM((5, 8, 128), jnp.int32),
            pltpu.SMEM((5, 8, 128), jnp.int32),
            pltpu.VMEM((2 * TILES, R, RHS), BF),
            pltpu.VMEM((PAIRS + 1, R, RHS), BF),
            pltpu.VMEM((CHUNKS, GROUP, TILES, PIECE, RHS), BF),
            pltpu.VMEM((CHUNKS, GROUP, TILES, PIECE, RHS), BF),
            pltpu.VMEM((CHUNKS, GROUP, TILES, PIECE, RHS), BF),
            pltpu.VMEM((CHUNKS, GROUP, TILES, PIECE, RHS), BF),
            pltpu.VMEM((CHUNKS, GROUP, R, RHS), BF),
            pltpu.VMEM((CHUNKS, GROUP, R, RHS), BF),
            pltpu.VMEM((BOX, R, RHS), BF),
            pltpu.SemaphoreType.DMA((4,)),
            pltpu.SemaphoreType.DMA((4,)),
            pltpu.SemaphoreType.DMA((5,)),
            pltpu.SemaphoreType.DMA((TILES,)),
            pltpu.SemaphoreType.DMA((GROUP,)),
            pltpu.SemaphoreType.DMA((GROUP,)),
            pltpu.SemaphoreType.DMA((3, CHUNKS, GROUP)),
            pltpu.SemaphoreType.DMA((3, CHUNKS, GROUP)),
        ],
        compiler_params=pltpu.CompilerParams(
            collective_id=0, has_side_effects=True, vmem_limit_bytes=48 << 20
        ),
        cost_estimate=pl.CostEstimate(flops=flops, bytes_accessed=5 << 20, transcendentals=0),
        name="butterfly",
    )(
        charges,
        pairs_a.T,
        pairs_b.T,
        pairs_c.T,
        mats_a,
        mats_b,
        mats_c,
        box_owner.reshape(1, BOX),
    )


def solution(mesh):
    both = ("wide", "narrow")
    placed = (
        P(both, None, None),
        P(both, None),
        P(both, None),
        P(both, None),
        P(both, None, None),
        P(both, None, None),
        P(both, None, None),
        P("wide", "narrow", None),
    )
    return jax.shard_map(
        per_device,
        mesh=mesh,
        in_specs=placed,
        out_specs=P(both, None, None),
        check_vma=False,
    )
```

profile of v0, /device:TPU:97, one launch (start us, length us, event | category | flops | bytes accessed | tf_op | source)
XLA Modules:
  0.0 93.4 jit_solution(9342764616556900957)
XLA Ops:
  0.0 0.0 copy-start.6
  0.0 0.0 copy-start.5
  0.0 0.0 copy-start.4
  0.0 0.0 copy-start.7
  0.0 0.7 copy-done.6
  0.7 0.0 copy-done.5
  0.7 0.0 copy-done.4
  0.7 0.0 copy-done.7
  0.7 0.0 copy-start
  0.7 1.2 %copy-done = bf16[16,256,128]{2,1,0:T(8,128)(2,1)S(1)} copy-done((bf16[16,256,128]{2,1,0:T(8,128)(2,1)S(1)}, bf16[16,256,128]{2,1,0:T(8,128)(2,1)}, u32[]{:S(2)}) %copy-start) | copy-done | bytes 1048600
  1.9 0.0 copy-start.1
  1.9 1.2 %copy-done.1 = bf16[8,256,256]{2,1,0:T(8,128)(2,1)S(1)} copy-done((bf16[8,256,256]{2,1,0:T(8,128)(2,1)S(1)}, bf16[8,256,256]{2,1,0:T(8,128)(2,1)}, u32[]{:S(2)}) %copy-start.1) | copy-done | bytes 1048600
  3.2 0.0 copy-start.2
  3.2 1.2 %copy-done.2 = bf16[8,256,256]{2,1,0:T(8,128)(2,1)S(1)} copy-done((bf16[8,256,256]{2,1,0:T(8,128)(2,1)S(1)}, bf16[8,256,256]{2,1,0:T(8,128)(2,1)}, u32[]{:S(2)}) %copy-start.2) | copy-done | bytes 1048600
  4.4 0.0 copy-start.3
  4.4 1.2 %copy-done.3 = bf16[8,256,256]{2,1,0:T(8,128)(2,1)S(1)} copy-done((bf16[8,256,256]{2,1,0:T(8,128)(2,1)S(1)}, bf16[8,256,256]{2,1,0:T(8,128)(2,1)}, u32[]{:S(2)}) %copy-start.3) | copy-done | bytes 1048600
  5.6 86.8 %butterfly.1 = bf16[16,256,128]{2,1,0:T(8,128)(2,1)S(1)} custom-call(bf16[16,256,128]{2,1,0:T(8,128)(2,1)S(1)} %copy-done, s32[4,64]{1,0:T(4,128)S(1)} %bitcast.4, s32[4,64]{1,0:T(4,128)S(1)} %bitcast.5, s32[4,64]{1,0:T(4,128)S(1)} %bitcast.6, bf16[8,256,256]{2,1,0:T(8,128)(2,1)S(1)} %copy-done.1, bf16[8,256,256]{2,1,0:T(8,128)(2,1)S(1)} %copy-done.2, ...), custom_call_target="tpu_custom_call" | custom-call | flops 3221225472 | bytes 5242880 | tf_op jit(solution)/shard_map/butterfly/pallas_call | solution.py:365
  92.4 1.0 %copy.10 = bf16[16,256,128]{2,1,0:T(8,128)(2,1)} copy(bf16[16,256,128]{2,1,0:T(8,128)(2,1)S(1)} %butterfly.1) | data formatting | bytes 2097152
Async XLA Ops:
  0.0 0.7 copy-start.6
  0.0 0.7 copy-start.5
  0.0 0.7 copy-start.4
  0.0 0.7 copy-start.7
  0.7 1.2 %copy-start = (bf16[16,256,128]{2,1,0:T(8,128)(2,1)S(1)}, bf16[16,256,128]{2,1,0:T(8,128)(2,1)}, u32[]{:S(2)}) copy-start(bf16[16,256,128]{2,1,0:T(8,128)(2,1)} %charges.1) | copy-start | bytes 3145732
  1.9 1.2 %copy-start.1 = (bf16[8,256,256]{2,1,0:T(8,128)(2,1)S(1)}, bf16[8,256,256]{2,1,0:T(8,128)(2,1)}, u32[]{:S(2)}) copy-start(bf16[8,256,256]{2,1,0:T(8,128)(2,1)} %mats_a.1) | copy-start | bytes 3145732
  3.2 1.2 %copy-start.2 = (bf16[8,256,256]{2,1,0:T(8,128)(2,1)S(1)}, bf16[8,256,256]{2,1,0:T(8,128)(2,1)}, u32[]{:S(2)}) copy-start(bf16[8,256,256]{2,1,0:T(8,128)(2,1)} %mats_b.1) | copy-start | bytes 3145732
  4.4 1.2 %copy-start.3 = (bf16[8,256,256]{2,1,0:T(8,128)(2,1)S(1)}, bf16[8,256,256]{2,1,0:T(8,128)(2,1)}, u32[]{:S(2)}) copy-start(bf16[8,256,256]{2,1,0:T(8,128)(2,1)} %mats_c.1) | copy-start | bytes 3145732
where the time goes:
time: 93.7 us; the launch traced here: 93.4 us
  Pallas kernels  86.8 us (93%)
  local copies, waits for them, and re-layouts  6.57 us (7%)
    pallas_call x1, Pallas kernels, per_device(): pl.pallas_call(body, out_shape=jax.ShapeDtypeStruct(charges.shape, charge...  86.8 us
    unnamed x17, local copies, waits for them, and re-layouts  6.57 us

commit v1 on v0

v1 whole, which is shorter than its diff:
```python
import functools

import jax
import jax.numpy as jnp
from jax import lax
from jax.experimental import pallas as pl
from jax.experimental.pallas import tpu as pltpu
from jax.sharding import PartitionSpec as P

MESH = pl.DeviceIdType.MESH
R = 256
RHS = 128
BOX = 16
PAIRS = 64
TRANS = 8
GROUP = 16
PIECE = R // GROUP
CHUNKS = 4
LANES = RHS // CHUNKS
TILES = BOX // CHUNKS
PARTS = CHUNKS // 2
ROWS = R // PARTS
PAIRS_OUT = BOX // 2
SPLIT = 4
UNROLL = 32
BF = jnp.bfloat16
F32 = jnp.float32


def far_first(e):
    return 8 + jnp.where(lax.rem(e, 2) == 1, -((e + 1) // 2), e // 2)


def column_of(row, eye):
    return jnp.sum(jnp.where(eye, row, 0), axis=1, keepdims=True)


def list_table(rows, tiled):
    line = lax.broadcasted_iota(jnp.int32, (PAIRS, PAIRS), 0)
    lane = lax.broadcasted_iota(jnp.int32, (PAIRS, PAIRS), 1)
    eye = line == lane
    source, target, matrix, live = (rows[i : i + 1, :] for i in range(4))
    place = lax.broadcasted_iota(jnp.int32, (1, PAIRS), 1)
    group = jnp.where(live > 0, target, BOX)
    key = group * PAIRS + place
    turn = (target - source) & (CHUNKS - 1)
    place_of = source // CHUNKS + TILES * turn if tiled else source
    word = place_of | (matrix << 4)
    key_col = column_of(key, eye)
    word_col = column_of(word, eye)
    group_col = key_col // PAIRS
    before = key < key_col
    rank_col = jnp.sum(jnp.where(before, 1, 0), axis=1, keepdims=True)
    follows = jnp.sum(jnp.where(before & (group == group_col), 1, 0), axis=1, keepdims=True)
    word_col = word_col | jnp.where((follows > 0) & (group_col < BOX), 1 << 7, 0)
    ordered = jnp.sum(jnp.where(rank_col == lane, word_col, 0), axis=0, keepdims=True)
    upto = jnp.sum(jnp.where(group_col <= lane, 1, 0), axis=0, keepdims=True)
    count = jnp.sum(jnp.where(group_col == lane, 1, 0), axis=0, keepdims=True)
    last = jnp.where(count > 0, upto - 1, PAIRS)
    return ordered, last


def send_table(row):
    line = lax.broadcasted_iota(jnp.int32, (BOX, BOX), 0)
    lane = lax.broadcasted_iota(jnp.int32, (BOX, BOX), 1)
    eye = line == lane
    col = column_of(row, eye)
    earlier = jnp.sum(jnp.where((row == col) & (lane < line), 1, 0), axis=1, keepdims=True)
    slot = 2 * col + earlier
    wide = lax.broadcasted_iota(jnp.int32, (BOX, PAIRS), 1)
    box = lax.broadcasted_iota(jnp.int32, (BOX, PAIRS), 0)
    return jnp.sum(jnp.where(slot == wide, box, 0), axis=0, keepdims=True)


def arrival_table(owners, me):
    hands = jnp.sum(jnp.where(owners == me, 1, 0), axis=1, keepdims=True)
    line = lax.broadcasted_iota(jnp.int32, (GROUP, GROUP), 0)
    lane = lax.broadcasted_iota(jnp.int32, (GROUP, GROUP), 1)
    filled = jnp.where(hands > 0, 1, 0)
    filled_row = jnp.sum(jnp.where(line == lane, filled, 0), axis=0, keepdims=True)
    rank = jnp.sum(jnp.where(lane < line, filled_row, 0), axis=1, keepdims=True)
    wide = lax.broadcasted_iota(jnp.int32, (GROUP, PAIRS), 1)
    index = lax.broadcasted_iota(jnp.int32, (GROUP, PAIRS), 0)
    return jnp.sum(jnp.where((filled > 0) & (rank == wide), index, 0), axis=0, keepdims=True)


def turned(x, groups):
    if isinstance(groups, int):
        return x if groups % CHUNKS == 0 else pltpu.roll(x, (groups % CHUNKS) * LANES, 1)
    return pltpu.roll(x, (groups & (CHUNKS - 1)) * LANES, 1)


def body(
    charges, pairs_a, pairs_b, pairs_c, mats_a, mats_b, mats_c, owner, out,
    c_v, m_a, m_b, m_c, lists, own_in, own_all, tables, table_s, arrival_s,
    x_v, p_v, stage_a, recv_a, stage_b, recv_b, stage_c, *rest,
):
    recv_c = rest[:CHUNKS]
    out_v, in_sem, late_sem, small_sem, table_sem, out_sem, own_send, own_recv, send_sem, recv_sem = rest[CHUNKS:]
    w = lax.axis_index("wide")
    n = lax.axis_index("narrow")
    barrier = pltpu.get_barrier_semaphore()

    def greet(d, carry):
        pl.semaphore_signal(
            barrier, inc=1, device_id=(w, lax.rem(n + d, GROUP)), device_id_type=MESH
        )
        pl.semaphore_signal(
            barrier, inc=1, device_id=(lax.rem(w + d, GROUP), n), device_id_type=MESH
        )
        return carry

    small = [
        pltpu.make_async_copy(src, lists.at[i], small_sem.at[i])
        for i, src in enumerate((pairs_a, pairs_b, pairs_c))
    ]
    small.append(pltpu.make_async_copy(owner, own_in, small_sem.at[3]))
    first_in = []
    for i, (src, dst) in enumerate(((charges, c_v), (mats_a, m_a))):
        size = src.shape[0] // SPLIT
        for k in range(SPLIT):
            span = pl.ds(k * size, size)
            first_in.append(
                pltpu.make_async_copy(src.at[span], dst.at[span], in_sem.at[i, k])
            )
    late_in = [
        pltpu.make_async_copy(mats_b, m_b, late_sem.at[0]),
        pltpu.make_async_copy(mats_c, m_c, late_sem.at[1]),
    ]
    for copy in small:
        copy.start()
    for copy in first_in:
        copy.start()
    lax.fori_loop(1, GROUP, greet, 0)

    table_copies = [
        pltpu.make_async_copy(tables.at[i], table_s.at[i], table_sem.at[i]) for i in range(4)
    ]
    arrival_copy = pltpu.make_async_copy(tables.at[4], arrival_s, table_sem.at[4])
    for copy in small:
        copy.wait()

    def list_of(level):
        ordered, last = list_table(lists[level], level > 0)
        tables[level, 0:1, 0:PAIRS] = ordered
        tables[level, 1:2, 0:PAIRS] = last
        table_copies[level].start()

    list_of(0)
    list_of(1)
    list_of(2)
    tables[3, 0:1, 0:PAIRS] = send_table(own_in[...])
    table_copies[3].start()
    own_all[w] = jnp.full((8, 128), -1, jnp.int32)
    own_all[w, 0:1, 0:BOX] = own_in[...]
    p_v[PAIRS] = jnp.zeros((R, RHS), BF)
    group = lax.broadcasted_iota(jnp.int32, (R, RHS), 1) // LANES

    def side_by_side(parts):
        tile = parts[0]
        for g in range(1, CHUNKS):
            tile = jnp.where(group[: tile.shape[0]] == g, parts[g], tile)
        return tile

    def narrow_copy(chunk, d):
        to = lax.rem(n + d, GROUP)
        return pltpu.make_async_remote_copy(
            src_ref=stage_a.at[chunk, to],
            dst_ref=recv_a.at[chunk, n],
            send_sem=send_sem.at[0, chunk, d],
            recv_sem=recv_sem.at[0, chunk, d],
            device_id=(w, to),
            device_id_type=MESH,
        )

    def wide_copy(phase, chunk, d):
        to = lax.rem(w + d, GROUP)
        stage, recv = ((stage_b, recv_b.at[chunk]), (stage_c, recv_c[chunk]))[phase - 1]
        return pltpu.make_async_remote_copy(
            src_ref=stage.at[chunk, to],
            dst_ref=recv.at[w],
            send_sem=send_sem.at[phase, chunk, d],
            recv_sem=recv_sem.at[phase, chunk, d],
            device_id=(to, n),
            device_id_type=MESH,
        )

    copies = (
        narrow_copy,
        functools.partial(wide_copy, 1),
        functools.partial(wide_copy, 2),
    )

    def owner_copy(d):
        to = lax.rem(w + d, GROUP)
        return pltpu.make_async_remote_copy(
            src_ref=own_all.at[w],
            dst_ref=own_all.at[w],
            send_sem=own_send.at[d],
            recv_sem=own_recv.at[d],
            device_id=(to, n),
            device_id_type=MESH,
        )

    def loop(low, high, step):
        def one(i, carry):
            step(i)
            return carry

        lax.fori_loop(low, high, one, 0)

    def load_received(recv, chunk):
        def step(i):
            tile = recv[chunk, :, i].reshape(R, RHS)
            for v in range(CHUNKS):
                x_v[v * TILES + i] = turned(tile, v)

        loop(0, TILES, step)

    def translate(level):
        matrices = (m_a, m_b, m_c)[level]
        sources = c_v if level == 0 else x_v

        def one(r, acc):
            word = table_s[level, 0, r]
            product = jnp.dot(
                matrices[(word >> 4) & 7], sources[word & 15], preferred_element_type=F32
            )
            acc = jnp.where((word >> 7) & 1 == 1, acc, 0.0) + product
            p_v[r] = acc.astype(BF)
            return acc

        lax.fori_loop(0, PAIRS, one, jnp.zeros((R, RHS), F32), unroll=UNROLL)

    def assemble(level, chunk):
        stage = (stage_a, stage_b)[level]

        def step(i):
            parts = []
            for g in range(CHUNKS):
                box = p_v[table_s[level, 1, CHUNKS * i + g]]
                parts.append(turned(box, g - chunk) if level == 0 else box)
            stage[chunk, :, i] = side_by_side(parts).reshape(GROUP, PIECE, RHS)

        loop(0, TILES, step)

    def send(level, chunk):
        loop(0, GROUP - 1, lambda e: copies[level](chunk, far_first(e)).start())
        if level == 0:
            recv_a[chunk, n] = stage_a[chunk, n]
        else:
            recv_b[chunk, w] = stage_b[chunk, w]

    def arrive(level, chunk):
        loop(1, GROUP, lambda d: copies[level](chunk, d).wait_recv())

    def sent(level, chunk):
        loop(1, GROUP, lambda d: copies[level](chunk, d).wait_send())

    def packet(chunk, to):
        parts = []
        for c in range(2):
            box = table_s[3, 0, 2 * to + c]
            slot = table_s[2, 1, box]
            for r in range(PARTS):
                rows = p_v[slot, r * ROWS : (r + 1) * ROWS]
                parts.append(turned(rows, c * PARTS + r - box))
        stage_c[chunk, to] = side_by_side(parts)

    def hand(chunk, low, high, pack=True, start=True):
        def step(e):
            d = far_first(e)
            if pack:
                packet(chunk, lax.rem(w + d, GROUP))
            if start:
                copies[2](chunk, d).start()

        loop(low, high, step)

    def keep(chunk):
        packet(chunk, w)
        recv_c[chunk][w] = stage_c[chunk, w]

    def place(j):
        span = pl.ds(2 * j, 2)
        return pltpu.make_async_copy(out_v.at[span], out.at[span], out_sem.at[j])

    def finish(chunk):
        def step(j):
            packed = recv_c[chunk][arrival_s[0, j]]
            lanes = slice(chunk * LANES, (chunk + 1) * LANES)
            for c in range(2):
                for r in range(PARTS):
                    rows = turned(packed, chunk - (c * PARTS + r))
                    out_v[2 * j + c, r * ROWS : (r + 1) * ROWS, lanes] = rows[:, lanes]
            if chunk == CHUNKS - 1:
                place(j).start()

        loop(0, PAIRS_OUT, step)

    def level_two(chunk):
        load_received(recv_a, chunk)
        translate(1)
        assemble(1, chunk)
        send(1, chunk)

    def level_three(chunk):
        load_received(recv_b, chunk)
        translate(2)

    table_copies[0].wait()
    for copy in first_in:
        copy.wait()
    for copy in late_in:
        copy.start()
    translate(0)
    assemble(0, 0)
    pl.semaphore_wait(barrier, 2 * (GROUP - 1))
    send(0, 0)
    loop(1, GROUP, lambda d: owner_copy(d).start())
    for chunk in range(1, CHUNKS):
        assemble(0, chunk)
    for copy in table_copies[1:4]:
        copy.wait()
    for copy in late_in:
        copy.wait()
    loop(1, GROUP, lambda d: owner_copy(d).wait())
    tables[4, 0:1, 0:PAIRS] = arrival_table(own_all[:, 0, 0:BOX], w)
    arrival_copy.start()
    arrival_copy.wait()

    arrive(0, 0)
    send(0, 1)
    level_two(0)
    arrive(0, 1)
    send(0, 2)
    level_two(1)
    arrive(1, 0)
    level_three(0)
    hand(0, 0, 15)
    keep(0)
    arrive(0, 2)
    send(0, 3)
    level_two(2)
    arrive(1, 1)
    level_three(1)
    hand(1, 0, 7)
    hand(1, 7, 15, start=False)
    keep(1)
    arrive(0, 3)
    level_two(3)
    hand(1, 7, 15, pack=False)
    arrive(1, 2)
    level_three(2)
    hand(2, 0, 7)
    hand(2, 7, 15, start=False)
    keep(2)
    arrive(1, 3)
    hand(2, 7, 15, pack=False)
    level_three(3)
    hand(3, 0, 15)
    keep(3)

    for level in range(2):
        for chunk in range(CHUNKS):
            sent(level, chunk)
    for chunk in range(CHUNKS):
        arrive(2, chunk)
        finish(chunk)
    loop(0, PAIRS_OUT, lambda j: place(j).wait())
    for chunk in range(CHUNKS):
        sent(2, chunk)


def per_device(charges, pairs_a, pairs_b, pairs_c, mats_a, mats_b, mats_c, box_owner):
    in_hbm = pl.BlockSpec(memory_space=pltpu.HBM)
    flops = 2 * 3 * PAIRS * R * R * RHS
    return pl.pallas_call(
        body,
        out_shape=jax.ShapeDtypeStruct(charges.shape, charges.dtype),
        in_specs=[in_hbm] * 8,
        out_specs=in_hbm,
        scratch_shapes=[
            pltpu.VMEM((BOX, R, RHS), BF),
            *[pltpu.VMEM((TRANS, R, R), BF)] * 3,
            pltpu.VMEM((3, 4, PAIRS), jnp.int32),
            pltpu.VMEM((1, BOX), jnp.int32),
            pltpu.VMEM((GROUP, 8, 128), jnp.int32),
            pltpu.VMEM((5, 8, 128), jnp.int32),
            pltpu.SMEM((4, 8, 128), jnp.int32),
            pltpu.SMEM((8, 128), jnp.int32),
            pltpu.VMEM((BOX, R, RHS), BF),
            pltpu.VMEM((PAIRS + 1, R, RHS), BF),
            *[pltpu.VMEM((CHUNKS, GROUP, TILES, PIECE, RHS), BF)] * 4,
            pltpu.VMEM((CHUNKS, GROUP, ROWS, RHS), BF),
            *[pltpu.VMEM((GROUP, ROWS, RHS), BF)] * CHUNKS,
            pltpu.VMEM((BOX, R, RHS), BF),
            pltpu.SemaphoreType.DMA((2, SPLIT)),
            pltpu.SemaphoreType.DMA((2,)),
            pltpu.SemaphoreType.DMA((4,)),
            pltpu.SemaphoreType.DMA((5,)),
            pltpu.SemaphoreType.DMA((PAIRS_OUT,)),
            pltpu.SemaphoreType.DMA((GROUP,)),
            pltpu.SemaphoreType.DMA((GROUP,)),
            pltpu.SemaphoreType.DMA((3, CHUNKS, GROUP)),
            pltpu.SemaphoreType.DMA((3, CHUNKS, GROUP)),
        ],
        compiler_params=pltpu.CompilerParams(
            collective_id=0, has_side_effects=True, vmem_limit_bytes=62 << 20
        ),
        cost_estimate=pl.CostEstimate(flops=flops, bytes_accessed=5 << 20, transcendentals=0),
        name="butterfly",
    )(
        charges,
        pairs_a.T,
        pairs_b.T,
        pairs_c.T,
        mats_a,
        mats_b,
        mats_c,
        box_owner.reshape(1, BOX),
    )


def solution(mesh):
    both = ("wide", "narrow")
    placed = (
        P(both, None, None),
        P(both, None),
        P(both, None),
        P(both, None),
        P(both, None, None),
        P(both, None, None),
        P(both, None, None),
        P("wide", "narrow", None),
    )
    return jax.shard_map(
        per_device,
        mesh=mesh,
        in_specs=placed,
        out_specs=P(both, None, None),
        check_vma=False,
    )
```

time: 93.7 us -> 76.6 us (0.82)
  the two profiles are of different devices: /device:TPU:97 before, /device:TPU:1 now
where the time goes in v1:
time: 76.6 us; the launch traced here: 76.4 us
  Pallas kernels  74.1 us (97%)
  local copies, waits for them, and re-layouts  2.3 us (3%)
    pallas_call x1, Pallas kernels, per_device(): pl.pallas_call(body, out_shape=jax.ShapeDtypeStruct(charges.shape, charge...  74.1 us
    unnamed x1, local copies, waits for them, and re-layouts  2.3 us

profile of v1, /device:TPU:1, one launch (start us, length us, event | category | flops | bytes accessed | tf_op | source)
XLA Modules:
  0.0 76.4 jit_solution(4655189808359653156)
XLA Ops:
  0.0 74.1 %butterfly.1 = bf16[16,256,128]{2,1,0:T(8,128)(2,1)} custom-call(bf16[16,256,128]{2,1,0:T(8,128)(2,1)} %charges.1, s32[4,64]{1,0:T(4,128)} %bitcast.4, s32[4,64]{1,0:T(4,128)} %bitcast.5, s32[4,64]{1,0:T(4,128)} %bitcast.6, bf16[8,256,256]{2,1,0:T(8,128)(2,1)} %mats_a.1, bf16[8,256,256]{2,1,0:T(8,128)(2,1)} %mats_b.1, bf16[8,256,256]{2,1,0:T(8,128)(2,1)} %mats_c.1, ...), custom_call_target="tpu_custom_call" | custom-call | flops 3221225472 | bytes 5242880 | tf_op jit(solution)/shard_map/butterfly/pallas_call | solution.py:378
  74.1 2.3 %copy.10 = bf16[16,256,128]{2,1,0:T(8,128)(2,1)} copy(bf16[16,256,128]{2,1,0:T(8,128)(2,1)} %butterfly.1) | data formatting | bytes 2097152

commit v2 on v1

--- a/solution.py
+++ b/solution.py
@@ -29,6 +29,27 @@
 
 def far_first(e):
     return 8 + jnp.where(lax.rem(e, 2) == 1, -((e + 1) // 2), e // 2)
+
+
+NEAR = tuple(
+    4 * dy + dx
+    for dy, dx in (
+        (0, 1), (0, 3), (1, 0), (3, 0), (0, 2), (2, 0), (1, 1), (3, 3),
+        (1, 3), (3, 1), (1, 2), (3, 2), (2, 1), (2, 3), (2, 2),
+    )
+)
+
+
+def listed(order, e):
+    low = sum(d << (4 * i) for i, d in enumerate(order[:7]))
+    high = sum(d << (4 * i) for i, d in enumerate(order[7:14]))
+    first = (jnp.int32(low) >> (4 * jnp.minimum(e, 6))) & 15
+    later = (jnp.int32(high) >> (4 * jnp.clip(e - 7, 0, 6))) & 15
+    return jnp.where(e < 7, first, jnp.where(e < 14, later, order[14]))
+
+
+def on_torus(w, d):
+    return ((w // 4 + d // 4) & 3) * 4 + ((w + d) & 3)
 
 
 def column_of(row, eye):
@@ -147,10 +168,6 @@
         table_copies[level].start()
 
     list_of(0)
-    list_of(1)
-    list_of(2)
-    tables[3, 0:1, 0:PAIRS] = send_table(own_in[...])
-    table_copies[3].start()
     own_all[w] = jnp.full((8, 128), -1, jnp.int32)
     own_all[w, 0:1, 0:BOX] = own_in[...]
     p_v[PAIRS] = jnp.zeros((R, RHS), BF)
@@ -174,7 +191,7 @@
         )
 
     def wide_copy(phase, chunk, d):
-        to = lax.rem(w + d, GROUP)
+        to = on_torus(w, d)
         stage, recv = ((stage_b, recv_b.at[chunk]), (stage_c, recv_c[chunk]))[phase - 1]
         return pltpu.make_async_remote_copy(
             src_ref=stage.at[chunk, to],
@@ -245,7 +262,7 @@
         loop(0, TILES, step)
 
     def send(level, chunk):
-        loop(0, GROUP - 1, lambda e: copies[level](chunk, far_first(e)).start())
+        loop(0, GROUP - 1, lambda e: copies[level](chunk, far_first(e) if level == 0 else listed(NEAR[::-1], e)).start())
         if level == 0:
             recv_a[chunk, n] = stage_a[chunk, n]
         else:
@@ -269,9 +286,9 @@
 
     def hand(chunk, low, high, pack=True, start=True):
         def step(e):
-            d = far_first(e)
+            d = listed(NEAR[::-1], e)
             if pack:
-                packet(chunk, lax.rem(w + d, GROUP))
+                packet(chunk, on_torus(w, d))
             if start:
                 copies[2](chunk, d).start()
 
@@ -318,6 +335,10 @@
     pl.semaphore_wait(barrier, 2 * (GROUP - 1))
     send(0, 0)
     loop(1, GROUP, lambda d: owner_copy(d).start())
+    list_of(1)
+    list_of(2)
+    tables[3, 0:1, 0:PAIRS] = send_table(own_in[...])
+    table_copies[3].start()
     for chunk in range(1, CHUNKS):
         assemble(0, chunk)
     for copy in table_copies[1:4]:
@@ -329,41 +350,40 @@
     arrival_copy.start()
     arrival_copy.wait()
 
+    sent(0, 0)
+    send(0, 1)
     arrive(0, 0)
-    send(0, 1)
     level_two(0)
+    sent(0, 1)
+    send(0, 2)
     arrive(0, 1)
-    send(0, 2)
     level_two(1)
     arrive(1, 0)
     level_three(0)
     hand(0, 0, 15)
     keep(0)
+    sent(0, 2)
+    send(0, 3)
     arrive(0, 2)
-    send(0, 3)
     level_two(2)
     arrive(1, 1)
     level_three(1)
-    hand(1, 0, 7)
-    hand(1, 7, 15, start=False)
+    hand(1, 0, 15)
     keep(1)
     arrive(0, 3)
     level_two(3)
-    hand(1, 7, 15, pack=False)
     arrive(1, 2)
     level_three(2)
-    hand(2, 0, 7)
-    hand(2, 7, 15, start=False)
+    hand(2, 0, 15)
     keep(2)
     arrive(1, 3)
-    hand(2, 7, 15, pack=False)
     level_three(3)
     hand(3, 0, 15)
     keep(3)
-
-    for level in range(2):
-        for chunk in range(CHUNKS):
-            sent(level, chunk)
+    sent(0, 3)
+
+    for chunk in range(CHUNKS):
+        sent(1, chunk)
     for chunk in range(CHUNKS):
         arrive(2, chunk)
         finish(chunk)

time: 76.6 us -> 73.5 us (0.960)
  Pallas kernels: 74.1 us -> 71 us
    pallas_call x1, Pallas kernels: 74.1 us -> 71 us  [per_device(): pl.pallas_call(body, out_shape=jax.ShapeDtypeStruct(charges.shape, charge...]
where the time goes in v2:
time: 73.5 us; the launch traced here: 73.4 us
  Pallas kernels  71 us (97%)
  local copies, waits for them, and re-layouts  2.3 us (3%)
    pallas_call x1, Pallas kernels, per_device(): pl.pallas_call(body, out_shape=jax.ShapeDtypeStruct(charges.shape, charge...  71 us
    unnamed x1, local copies, waits for them, and re-layouts  2.3 us

profile of v2, /device:TPU:1, one launch (start us, length us, event | category | flops | bytes accessed | tf_op | source)
XLA Modules:
  0.0 73.4 jit_solution(3141251950109910892)
XLA Ops:
  0.0 71.0 %butterfly.1 = bf16[16,256,128]{2,1,0:T(8,128)(2,1)} custom-call(bf16[16,256,128]{2,1,0:T(8,128)(2,1)} %charges.1, s32[4,64]{1,0:T(4,128)} %bitcast.4, s32[4,64]{1,0:T(4,128)} %bitcast.5, s32[4,64]{1,0:T(4,128)} %bitcast.6, bf16[8,256,256]{2,1,0:T(8,128)(2,1)} %mats_a.1, bf16[8,256,256]{2,1,0:T(8,128)(2,1)} %mats_b.1, bf16[8,256,256]{2,1,0:T(8,128)(2,1)} %mats_c.1, ...), custom_call_target="tpu_custom_call" | custom-call | flops 3221225472 | bytes 5242880 | tf_op jit(solution)/shard_map/butterfly/pallas_call | solution.py:398
  71.1 2.3 %copy.10 = bf16[16,256,128]{2,1,0:T(8,128)(2,1)} copy(bf16[16,256,128]{2,1,0:T(8,128)(2,1)} %butterfly.1) | data formatting | bytes 2097152

commit v3 on v2

--- a/solution.py
+++ b/solution.py
@@ -31,21 +31,21 @@
     return 8 + jnp.where(lax.rem(e, 2) == 1, -((e + 1) // 2), e // 2)
 
 
-NEAR = tuple(
+FAR_FIRST = tuple(
     4 * dy + dx
     for dy, dx in (
-        (0, 1), (0, 3), (1, 0), (3, 0), (0, 2), (2, 0), (1, 1), (3, 3),
-        (1, 3), (3, 1), (1, 2), (3, 2), (2, 1), (2, 3), (2, 2),
+        (2, 2), (2, 3), (2, 1), (3, 2), (1, 2), (3, 1), (1, 3), (3, 3),
+        (1, 1), (2, 0), (0, 2), (3, 0), (1, 0), (0, 3), (0, 1),
     )
 )
 
 
-def listed(order, e):
-    low = sum(d << (4 * i) for i, d in enumerate(order[:7]))
-    high = sum(d << (4 * i) for i, d in enumerate(order[7:14]))
+def torus_far_first(e):
+    low = sum(d << (4 * i) for i, d in enumerate(FAR_FIRST[:7]))
+    high = sum(d << (4 * i) for i, d in enumerate(FAR_FIRST[7:14]))
     first = (jnp.int32(low) >> (4 * jnp.minimum(e, 6))) & 15
     later = (jnp.int32(high) >> (4 * jnp.clip(e - 7, 0, 6))) & 15
-    return jnp.where(e < 7, first, jnp.where(e < 14, later, order[14]))
+    return jnp.where(e < 7, first, jnp.where(e < 14, later, FAR_FIRST[14]))
 
 
 def on_torus(w, d):
@@ -117,7 +117,7 @@
     x_v, p_v, stage_a, recv_a, stage_b, recv_b, stage_c, *rest,
 ):
     recv_c = rest[:CHUNKS]
-    out_v, in_sem, late_sem, small_sem, table_sem, out_sem, own_send, own_recv, send_sem, recv_sem = rest[CHUNKS:]
+    in_sem, late_sem, small_sem, table_sem, own_send, own_recv, send_sem, recv_sem = rest[CHUNKS:]
     w = lax.axis_index("wide")
     n = lax.axis_index("narrow")
     barrier = pltpu.get_barrier_semaphore()
@@ -262,7 +262,7 @@
         loop(0, TILES, step)
 
     def send(level, chunk):
-        loop(0, GROUP - 1, lambda e: copies[level](chunk, far_first(e) if level == 0 else listed(NEAR[::-1], e)).start())
+        loop(0, GROUP - 1, lambda e: copies[level](chunk, far_first(e) if level == 0 else torus_far_first(e)).start())
         if level == 0:
             recv_a[chunk, n] = stage_a[chunk, n]
         else:
@@ -284,23 +284,15 @@
                 parts.append(turned(rows, c * PARTS + r - box))
         stage_c[chunk, to] = side_by_side(parts)
 
-    def hand(chunk, low, high, pack=True, start=True):
+    def hand(chunk):
         def step(e):
-            d = listed(NEAR[::-1], e)
-            if pack:
-                packet(chunk, on_torus(w, d))
-            if start:
-                copies[2](chunk, d).start()
-
-        loop(low, high, step)
-
-    def keep(chunk):
+            d = torus_far_first(e)
+            packet(chunk, on_torus(w, d))
+            copies[2](chunk, d).start()
+
+        loop(0, GROUP - 1, step)
         packet(chunk, w)
         recv_c[chunk][w] = stage_c[chunk, w]
-
-    def place(j):
-        span = pl.ds(2 * j, 2)
-        return pltpu.make_async_copy(out_v.at[span], out.at[span], out_sem.at[j])
 
     def finish(chunk):
         def step(j):
@@ -309,9 +301,7 @@
             for c in range(2):
                 for r in range(PARTS):
                     rows = turned(packed, chunk - (c * PARTS + r))
-                    out_v[2 * j + c, r * ROWS : (r + 1) * ROWS, lanes] = rows[:, lanes]
-            if chunk == CHUNKS - 1:
-                place(j).start()
+                    out[2 * j + c, r * ROWS : (r + 1) * ROWS, lanes] = rows[:, lanes]
 
         loop(0, PAIRS_OUT, step)
 
@@ -360,26 +350,22 @@
     level_two(1)
     arrive(1, 0)
     level_three(0)
-    hand(0, 0, 15)
-    keep(0)
+    hand(0)
     sent(0, 2)
     send(0, 3)
     arrive(0, 2)
     level_two(2)
     arrive(1, 1)
     level_three(1)
-    hand(1, 0, 15)
-    keep(1)
+    hand(1)
     arrive(0, 3)
     level_two(3)
     arrive(1, 2)
     level_three(2)
-    hand(2, 0, 15)
-    keep(2)
+    hand(2)
     arrive(1, 3)
     level_three(3)
-    hand(3, 0, 15)
-    keep(3)
+    hand(3)
     sent(0, 3)
 
     for chunk in range(CHUNKS):
@@ -387,8 +373,6 @@
     for chunk in range(CHUNKS):
         arrive(2, chunk)
         finish(chunk)
-    loop(0, PAIRS_OUT, lambda j: place(j).wait())
-    for chunk in range(CHUNKS):
         sent(2, chunk)
 
 
@@ -399,7 +383,7 @@
         body,
         out_shape=jax.ShapeDtypeStruct(charges.shape, charges.dtype),
         in_specs=[in_hbm] * 8,
-        out_specs=in_hbm,
+        out_specs=pl.BlockSpec(memory_space=pltpu.VMEM),
         scratch_shapes=[
             pltpu.VMEM((BOX, R, RHS), BF),
             *[pltpu.VMEM((TRANS, R, R), BF)] * 3,
@@ -414,31 +398,29 @@
             *[pltpu.VMEM((CHUNKS, GROUP, TILES, PIECE, RHS), BF)] * 4,
             pltpu.VMEM((CHUNKS, GROUP, ROWS, RHS), BF),
             *[pltpu.VMEM((GROUP, ROWS, RHS), BF)] * CHUNKS,
-            pltpu.VMEM((BOX, R, RHS), BF),
             pltpu.SemaphoreType.DMA((2, SPLIT)),
             pltpu.SemaphoreType.DMA((2,)),
             pltpu.SemaphoreType.DMA((4,)),
             pltpu.SemaphoreType.DMA((5,)),
-            pltpu.SemaphoreType.DMA((PAIRS_OUT,)),
             pltpu.SemaphoreType.DMA((GROUP,)),
             pltpu.SemaphoreType.DMA((GROUP,)),
             pltpu.SemaphoreType.DMA((3, CHUNKS, GROUP)),
             pltpu.SemaphoreType.DMA((3, CHUNKS, GROUP)),
         ],
         compiler_params=pltpu.CompilerParams(
-            collective_id=0, has_side_effects=True, vmem_limit_bytes=62 << 20
+            collective_id=0, has_side_effects=True, vmem_limit_bytes=50 << 20
         ),
         cost_estimate=pl.CostEstimate(flops=flops, bytes_accessed=5 << 20, transcendentals=0),
         name="butterfly",
     )(
-        charges,
-        pairs_a.T,
-        pairs_b.T,
-        pairs_c.T,
-        mats_a,
-        mats_b,
-        mats_c,
-        box_owner.reshape(1, BOX),
+        pltpu.with_memory_space_constraint(charges, pltpu.HBM),
+        pltpu.with_memory_space_constraint(pairs_a.T, pltpu.HBM),
+        pltpu.with_memory_space_constraint(pairs_b.T, pltpu.HBM),
+        pltpu.with_memory_space_constraint(pairs_c.T, pltpu.HBM),
+        pltpu.with_memory_space_constraint(mats_a, pltpu.HBM),
+        pltpu.with_memory_space_constraint(mats_b, pltpu.HBM),
+        pltpu.with_memory_space_constraint(mats_c, pltpu.HBM),
+        pltpu.with_memory_space_constraint(box_owner.reshape(1, BOX), pltpu.HBM),
     )
 
 

time: 73.5 us -> 71.1 us (0.967)
  local copies, waits for them, and re-layouts: 2.3 us -> 0.97 us
  Pallas kernels: 71 us -> 70 us
    unnamed x1, local copies, waits for them, and re-layouts: 2.3 us -> 0.97 us
    pallas_call x1, Pallas kernels: 71 us -> 70 us  [per_device(): pl.pallas_call(body, out_shape=jax.ShapeDtypeStruct(charges.shape, charge...]
where the time goes in v3:
time: 71.1 us; the launch traced here: 71 us
  Pallas kernels  70 us (98%)
  local copies, waits for them, and re-layouts  0.97 us (1%)
    pallas_call x1, Pallas kernels, per_device(): pl.pallas_call(body, out_shape=jax.ShapeDtypeStruct(charges.shape, charge...  70 us

profile of v3, /device:TPU:1, one launch (start us, length us, event | category | flops | bytes accessed | tf_op | source)
XLA Modules:
  0.0 71.0 jit_solution(4741811142957152048)
XLA Ops:
  0.0 70.0 %butterfly.1 = bf16[16,256,128]{2,1,0:T(8,128)(2,1)S(1)} custom-call(bf16[16,256,128]{2,1,0:T(8,128)(2,1)} %charges.1, s32[4,64]{1,0:T(4,128)} %bitcast.4, s32[4,64]{1,0:T(4,128)} %bitcast.5, s32[4,64]{1,0:T(4,128)} %bitcast.6, bf16[8,256,256]{2,1,0:T(8,128)(2,1)} %mats_a.1, bf16[8,256,256]{2,1,0:T(8,128)(2,1)} %mats_b.1, bf16[8,256,256]{2,1,0:T(8,128)(2,1)} %mats_c.1, ...), custom_call_target="tpu_custom_call" | custom-call | flops 3221225472 | bytes 5242880 | tf_op jit(solution)/shard_map/butterfly/pallas_call | solution.py:382
  70.0 1.0 %copy.10 = bf16[16,256,128]{2,1,0:T(8,128)(2,1)} copy(bf16[16,256,128]{2,1,0:T(8,128)(2,1)S(1)} %butterfly.1) | data formatting | bytes 2097152

commit v4 on v3

--- a/solution.py
+++ b/solution.py
@@ -350,9 +350,9 @@
     level_two(1)
     arrive(1, 0)
     level_three(0)
-    hand(0)
     sent(0, 2)
     send(0, 3)
+    hand(0)
     arrive(0, 2)
     level_two(2)
     arrive(1, 1)

time: 71.1 us -> 70.9 us (level)
  no operation moved by 1% of the time
where the time goes in v4:
time: 70.9 us; the launch traced here: 70.8 us
  Pallas kernels  69.8 us (98%)
  local copies, waits for them, and re-layouts  0.97 us (1%)
    pallas_call x1, Pallas kernels, per_device(): pl.pallas_call(body, out_shape=jax.ShapeDtypeStruct(charges.shape, charge...  69.8 us

profile of v4, /device:TPU:1, one launch (start us, length us, event | category | flops | bytes accessed | tf_op | source)
XLA Modules:
  0.0 70.8 jit_solution(16264236461199853428)
XLA Ops:
  0.0 69.8 %butterfly.1 = bf16[16,256,128]{2,1,0:T(8,128)(2,1)S(1)} custom-call(bf16[16,256,128]{2,1,0:T(8,128)(2,1)} %charges.1, s32[4,64]{1,0:T(4,128)} %bitcast.4, s32[4,64]{1,0:T(4,128)} %bitcast.5, s32[4,64]{1,0:T(4,128)} %bitcast.6, bf16[8,256,256]{2,1,0:T(8,128)(2,1)} %mats_a.1, bf16[8,256,256]{2,1,0:T(8,128)(2,1)} %mats_b.1, bf16[8,256,256]{2,1,0:T(8,128)(2,1)} %mats_c.1, ...), custom_call_target="tpu_custom_call" | custom-call | flops 3221225472 | bytes 5242880 | tf_op jit(solution)/shard_map/butterfly/pallas_call | solution.py:382
  69.8 1.0 %copy.10 = bf16[16,256,128]{2,1,0:T(8,128)(2,1)} copy(bf16[16,256,128]{2,1,0:T(8,128)(2,1)S(1)} %butterfly.1) | data formatting | bytes 2097152
